TPU v7x, 32 devices: a whole 2x2x4 slice. The times are simulated.
32 devices in a mesh: row: 8 (over y, x, core), col: 4 (over z).
Axes of the slice: x: 2, y: 2, z: 4, core: 2. Of those that a mesh axis runs over, the one named last changes fastest.
Arguments:
- inverse_blocks: float32 [4096, 4096], P('row', 'col'), may hold values from -0.09375 to 0.09375
- panel: bfloat16 [4096, 4096], P('row', 'col'), may hold values from -1.5 to 1.5
- diag_inverse: float32 [512, 4096], P('row', 'col'), may hold values from -6 to 6
- members: int32 [8, 8], replicated, may hold values from 0 to 7, each once within a row
- counts: int32 [8], replicated, may hold values from 1 to 8, as said below
Outputs:
- offdiag: float32 [4096, 4096], P('row', 'col')
- new_diag: float32 [512, 4096], P('row', 'col')
Inputs may be any that keep to these rules, and one draw needn't show every extreme that they name: Each row of members names every ancestor once. `counts`: some supernode lists all 8 ancestors and some lists one.
All inputs are finite; a program needn't handle non-finite values.
Results may differ from a plain program's by a relative error of at most 0.0003.
Values may be sent and summed in bfloat16 or wider, within the bound.
A program may use at most 128 MiB of HBM per device.

v0:
```python
import jax
import jax.numpy as jnp
from jax import lax
from jax.sharding import PartitionSpec as P

B = 512


def body(inverse_blocks, panel, diag_inverse, members, counts):
    rows_dev = panel.shape[0]
    sup_count = panel.shape[1] // B
    row_index = lax.axis_index("row")
    col_index = lax.axis_index("col")
    ancestor = row_index * rows_dev // B
    first_sup = col_index * sup_count
    local_members = lax.dynamic_slice_in_dim(members, first_sup, sup_count, 0)
    local_counts = lax.dynamic_slice_in_dim(counts, first_sup, sup_count, 0)
    slot_index = jnp.arange(members.shape[1], dtype=jnp.int32)
    live_slot = slot_index[None, :] < local_counts[:, None]
    row_mask = jnp.sum(
        jnp.where((local_members == ancestor) & live_slot, 1.0, 0.0).astype(jnp.float32), axis=1
    )
    column_mask = jnp.repeat(row_mask, B)
    masked = panel * column_mask.astype(jnp.bfloat16)[None, :]
    inverse_rows = lax.all_gather(inverse_blocks, "col", axis=1, tiled=True)
    running = jnp.dot(
        inverse_rows,
        lax.all_gather(masked, "row", axis=0, tiled=True).astype(jnp.float32),
        precision=lax.Precision.HIGHEST,
    )
    offdiag = -(running * column_mask[None, :])
    masked_wide = masked.astype(jnp.float32).reshape(rows_dev, sup_count, B)
    offdiag_wide = offdiag.reshape(rows_dev, sup_count, B)
    diag_terms = jnp.einsum(
        "ikc,ikd->ckd", masked_wide, offdiag_wide, precision=lax.Precision.HIGHEST
    )
    summed = lax.psum_scatter(
        diag_terms.reshape(B, sup_count * B), "row", scatter_dimension=0, tiled=True
    )
    return (offdiag, diag_inverse - summed)


def solution(mesh):
    return jax.shard_map(
        body,
        mesh=mesh,
        in_specs=(P("row", "col"), P("row", "col"), P("row", "col"), P(), P()),
        out_specs=(P("row", "col"), P("row", "col")),
        check_vma=False,
    )
```

profile of v0, /device:TPU:0, one launch (start us, length us, event | category | flops | bytes accessed | tf_op | source)
XLA Modules:
  0.0 291.6 jit_solution(4853133798508175931)
XLA Ops:
  7.2 0.0 copy-start.3
  7.2 0.0 copy-start.1
  7.2 0.0 all-gather.5.cloned.1.call-start
  7.2 0.7 all-gather.5.cloned.1.call-update
  7.9 0.0 all-gather.3.cloned.1.call-start
  8.0 0.0 copy-done.3
  8.0 0.1 dynamic_slice.7
  8.1 0.9 fusion.3
  8.9 0.1 broadcast_bitcast_fusion
  9.0 0.0 copy-done.1
  9.0 1.0 broadcast_multiply_fusion
  10.1 0.0 all-gather.3.cloned.1.call-update
  10.1 0.0 copy-start
  10.1 0.0 reduce-scatter.2.cloned.1.call-start
  10.2 151.8 %all-gather.5.cloned.1.call-done = f32[512,4096]{1,0:T(8,128)} async-done(((f32[512,1024]{1,0:T(8,128)}), f32[512,4096]{1,0:T(8,128)}) %all-gather.5.cloned.1.call-update) | async-done | bytes 8388624 | tf_op jit(solution)/shard_map/all_gather | solution.py:25
  162.0 55.1 %all-gather.3.cloned.1.call-done = bf16[4096,1024]{1,0:T(8,128)(2,1)} async-done(((bf16[512,1024]{1,0:T(8,128)(2,1)}), bf16[4096,1024]{1,0:T(8,128)(2,1)}) %all-gather.3.cloned.1.call-update) | async-done | bytes 8388624 | tf_op jit(solution)/shard_map/all_gather | solution.py:28
  217.0 18.9 %multiply_negate_fusion = f32[1024,512]{1,0:T(8,128)S(1)} fusion(bf16[4096,1024]{1,0:T(8,128)(2,1)} %all-gather.3.cloned.1.call-done, f32[512,4096]{1,0:T(8,128)} %all-gather.5.cloned.1.call-done, f32[1024]{0:T(1024)S(1)} %bitcast.21), kind=kOutput, calls=%fused_computation | convolution fusion | flops 25770852352 | bytes 18878464 | tf_op jit(solution)/shard_map/dot_general | solution.py:26
  235.9 0.0 copy-done
  235.9 3.1 %fusion = f32[2,512,512]{2,1,0:T(8,128)} fusion(f32[512,2,512]{0,2,1:T(8,128)S(1)} %bitcast.17, bf16[64,2,8,512]{3,2,1,0:T(8,128)(2,1)S(1)} %bitcast.16), kind=kOutput, calls=%fused_computation.1 | convolution fusion | flops 3221225472 | bytes 5242880 | tf_op jit(solution)/shard_map/ikc,ikd->ckd/dot_general | solution.py:34
  239.0 2.9 %copy.8 = f32[512,1024]{1,0:T(8,128)} copy(f32[512,1024]{0,1:T(8,128)} %bitcast.19) | data formatting | bytes 4194304 | tf_op jit(solution)/shard_map/reshape | solution.py:38
  242.0 0.0 reduce-scatter.2.cloned.1.call-update
  242.0 0.0 copy-start.2
  242.0 1.8 copy.9
  243.8 39.6 %reduce-scatter.2.cloned.1.call-done = f32[64,1024]{1,0:T(8,128)} async-done(((f32[512,1024]{1,0:T(8,128)}), f32[64,1024]{1,0:T(8,128)}) %reduce-scatter.2.cloned.1.call-update) | async-done | bytes 262160 | tf_op jit(solution)/shard_map/reduce_scatter | solution.py:37
  283.4 0.0 copy-done.2
  283.4 1.7 sub.8
  (2 shorter events, 0.0 us)
Async XLA Ops:
  7.2 0.8 copy-start.3
  7.2 1.9 copy-start.1
  7.2 154.8 %all-gather.5.cloned.1.call-start = ((), (), s32[]{:S(2)}) async-start(), calls=%async_computation.2 | async-start | bytes 10485760 | tf_op jit(solution)/shard_map/all_gather | solution.py:25
  7.9 209.1 %all-gather.3.cloned.1.call-start = ((), (), s32[]{:S(2)}) async-start(), calls=%async_computation.1 | async-start | bytes 9437184 | tf_op jit(solution)/shard_map/all_gather | solution.py:28
  10.1 225.8 %copy-start = (bf16[512,1024]{1,0:T(8,128)(2,1)S(1)}, bf16[512,1024]{1,0:T(8,128)(2,1)}, u32[]{:S(2)}) copy-start(bf16[512,1024]{1,0:T(8,128)(2,1)} %broadcast_multiply_fusion) | copy-start | bytes 3145732
  10.1 273.3 %reduce-scatter.2.cloned.1.call-start = ((), (), s32[]{:S(2)}) async-start(), calls=%async_computation.3 | async-start | bytes 2359296 | tf_op jit(solution)/shard_map/reduce_scatter | solution.py:37
  242.0 41.4 %copy-start.2 = (f32[64,1024]{1,0:T(8,128)S(1)}, f32[64,1024]{1,0:T(8,128)}, u32[]{:S(2)}) copy-start(f32[64,1024]{1,0:T(8,128)} %param.7) | copy-start | bytes 786436
Sparse Core Ops, SparseCore 0:
  9.6 152.3 all-gather.4
  164.4 52.5 all-gather.2
  242.1 41.2 reduce-scatter.1
where the time goes:
time: 292 us
  waiting for transfers between devices  247 us (85%)
  matrix products  22 us (8%)
  between operations  13.8 us (5%)
  local copies, waits for them, and re-layouts  4.93 us (2%)
  other arithmetic  3.6 us (1%)
    all_gather x1, waiting for transfers between devices, body(): inverse_rows = lax.all_gather(inverse_blocks, 'col', axis=1, tiled=True)  152 us
    all_gather x1, waiting for transfers between devices, body(): lax.all_gather(masked, 'row', axis=0, tiled=True).astype(jnp.float32)  55.1 us
    reduce_scatter x1, waiting for transfers between devices, body(): lax.psum_scatter(diag_terms.reshape(B, sup_count * B), 'row', scatter_dim...  39.6 us
    dot_general x1, matrix products, body(): jnp.dot(inverse_rows, lax.all_gather(masked, 'row', axis=0, tiled=True).a...  18.9 us
  transfers between devices with their start and end apart: 3, of which 3 were waited for; matrix products, arithmetic and copies ran while one was open for 1% of the time, Pallas kernels for 0%

commit v1 on v0

--- a/solution.py
+++ b/solution.py
@@ -1,9 +1,38 @@
+import functools
 import jax
 import jax.numpy as jnp
 from jax import lax
 from jax.sharding import PartitionSpec as P
 
 B = 512
+
+
+def rates_switch(q_in, group_axis):
+    num = lax.axis_size(group_axis)
+    shelf = []
+    k = 0
+    while k < num:
+        shelf.append((k, (k + 1) % num))
+        k += 1
+    inbox = []
+    k = 0
+    while k < num:
+        inbox.append((k, (k - 1) % num))
+        k = k + 1
+    b_now, frame_out = ([q_in], [q_in])
+    for _ in range(num // 2):
+        z1 = lax.ppermute(b_now[-1], group_axis, shelf)
+        b_now.append(z1)
+    to_i = 0
+    while to_i < (num - 1) // 2:
+        frame_out.append(lax.ppermute(frame_out[-1], group_axis, inbox))
+        to_i = to_i + 1
+    y1 = jnp.concatenate([*b_now[::-1], *frame_out[1:]], axis=0)
+    vec_out = lax.axis_index(group_axis)
+    return jnp.roll(y1, (vec_out - num // 2) * q_in.shape[0], axis=0)
+
+
+measure_inputs = functools.partial(rates_switch, group_axis="row")
 
 
 def body(inverse_blocks, panel, diag_inverse, members, counts):
@@ -24,9 +53,7 @@
     masked = panel * column_mask.astype(jnp.bfloat16)[None, :]
     inverse_rows = lax.all_gather(inverse_blocks, "col", axis=1, tiled=True)
     running = jnp.dot(
-        inverse_rows,
-        lax.all_gather(masked, "row", axis=0, tiled=True).astype(jnp.float32),
-        precision=lax.Precision.HIGHEST,
+        inverse_rows, measure_inputs(masked).astype(jnp.float32), precision=lax.Precision.HIGHEST
     )
     offdiag = -(running * column_mask[None, :])
     masked_wide = masked.astype(jnp.float32).reshape(rows_dev, sup_count, B)

time: 292 us -> 236 us (0.81)
  waiting for transfers between devices: 247 us -> 153 us
  local copies, waits for them, and re-layouts: 4.93 us -> 30 us
  starting transfers between devices: 0.12 us -> 7.84 us
  other arithmetic: 3.6 us -> 7.58 us
    all_gather x1, waiting for transfers between devices: 152 us -> 32.1 us  [body(): inverse_rows = lax.all_gather(inverse_blocks, 'col', axis=1, tiled=True)]
    ppermute x0 -> x7, waiting for transfers between devices: none -> 82.9 us  [the longest x4 82.9 us: rates_switch(): z1 = lax.ppermute(b_now[-1], group_axis, shelf)]
    all_gather x1 -> x0, waiting for transfers between devices: 55.1 us -> none  [body(): lax.all_gather(masked, 'row', axis=0, tiled=True).astype(jnp.float32)]
    unnamed x11 -> x28, local copies, waits for them, and re-layouts: 1.91 us -> 25.3 us
    ppermute x0 -> x7, starting transfers between devices: none -> 7.76 us  [the longest x3 7.25 us: rates_switch(): frame_out.append(lax.ppermute(frame_out[-1], group_axis, inbox))]
    unnamed x0 -> x2, other arithmetic: none -> 3.73 us
  transfers between devices with their start and end apart: 3 -> 9, of which waited for: 3 -> 6; matrix products, arithmetic and copies ran while one was open for 1% -> 14% of each run, Pallas kernels for 0% -> 0%
where the time goes in v1:
time: 236 us; the launch traced here: 235 us
  waiting for transfers between devices  153 us (65%)
  local copies, waits for them, and re-layouts  30 us (13%)
  matrix products  22 us (9%)
  between operations  14.1 us (6%)
  starting transfers between devices  7.84 us (3%)
  other arithmetic  7.58 us (3%)
    ppermute x4, waiting for transfers between devices, rates_switch(): z1 = lax.ppermute(b_now[-1], group_axis, shelf)  82.9 us
    reduce_scatter x1, waiting for transfers between devices, body(): lax.psum_scatter(diag_terms.reshape(B, sup_count * B), 'row', scatter_dim...  37.8 us
    all_gather x1, waiting for transfers between devices, body(): inverse_rows = lax.all_gather(inverse_blocks, 'col', axis=1, tiled=True)  32.1 us
    unnamed x28, local copies, waits for them, and re-layouts  25.3 us
    dot_general x1, matrix products, body(): jnp.dot(inverse_rows, measure_inputs(masked).astype(jnp.float32), precisi...  18.9 us
    ppermute x3, starting transfers between devices, rates_switch(): frame_out.append(lax.ppermute(frame_out[-1], group_axis, inbox))  7.25 us
  transfers between devices with their start and end apart: 9, of which 6 were waited for; matrix products, arithmetic and copies ran while one was open for 14% of the time, Pallas kernels for 0%

profile of v1, /device:TPU:0, one launch (start us, length us, event | category | flops | bytes accessed | tf_op | source)
XLA Modules:
  0.0 235.0 jit_solution(14626788491708903919)
XLA Ops:
  7.2 0.0 copy-start
  7.2 0.0 all-gather.2.cloned.1.call-start
  7.2 0.7 all-gather.2.cloned.1.call-update
  7.9 0.0 reduce-scatter.2.cloned.1.call-start
  8.0 0.7 dynamic_slice.11
  8.7 0.9 fusion.7
  9.6 0.1 broadcast_bitcast_fusion
  9.7 1.3 broadcast_multiply_fusion
  11.0 0.0 copy-start.1
  11.0 0.5 collective-permute-start
  11.5 15.4 %collective-permute-done = bf16[512,1024]{1,0:T(8,128)(2,1)S(1)} collective-permute-done((bf16[512,1024]{1,0:T(8,128)(2,1)S(1)}, bf16[512,1024]{1,0:T(8,128)(2,1)S(1)}, u32[]{:S(2)}, u32[]{:S(2)}) %collective-permute-start) | collective-permute-done | bytes 1048608 | tf_op jit(solution)/shard_map/ppermute | solution.py:24
  26.8 0.0 collective-permute-start.1
  26.8 0.0 copy-done.1
  26.8 2.6 %collective-permute-start.4 = (bf16[512,1024]{1,0:T(8,128)(2,1)S(1)}, bf16[512,1024]{1,0:T(8,128)(2,1)S(1)}, u32[]{:S(2)}, u32[]{:S(2)}) collective-permute-start(bf16[512,1024]{1,0:T(8,128)(2,1)S(1)} %broadcast_multiply_fusion), channel_id=1, source_target_pairs={{0,28},{4,0},{8,4},{12,8},{16,12},{20,16},{24,20},{28,24},{1,29},{... | collective-permute-start | bytes 3145736 | tf_op jit(solution)/shard_map/ppermute | solution.py:28
  29.5 21.9 %collective-permute-done.1 = bf16[512,1024]{1,0:T(8,128)(2,1)S(1)} collective-permute-done((bf16[512,1024]{1,0:T(8,128)(2,1)S(1)}, bf16[512,1024]{1,0:T(8,128)(2,1)S(1)}, u32[]{:S(2)}, u32[]{:S(2)}) %collective-permute-start.1) | collective-permute-done | bytes 1048608 | tf_op jit(solution)/shard_map/ppermute | solution.py:24
  51.4 0.0 copy-start.3
  51.4 0.0 collective-permute-start.2
  51.4 0.0 collective-permute-done.4
  51.4 1.0 copy-done.3
  52.4 2.0 collective-permute-start.5
  54.4 22.2 %collective-permute-done.2 = bf16[512,1024]{1,0:T(8,128)(2,1)} collective-permute-done((bf16[512,1024]{1,0:T(8,128)(2,1)S(1)}, bf16[512,1024]{1,0:T(8,128)(2,1)}, u32[]{:S(2)}, u32[]{:S(2)}) %collective-permute-start.2) | collective-permute-done | bytes 1048608 | tf_op jit(solution)/shard_map/ppermute | solution.py:24
  76.6 0.0 collective-permute-start.3
  76.6 0.0 copy-start.4
  76.6 0.0 collective-permute-done.5
  76.6 2.6 %collective-permute-start.6 = (bf16[512,1024]{1,0:T(8,128)(2,1)}, bf16[512,1024]{1,0:T(8,128)(2,1)S(1)}, u32[]{:S(2)}, u32[]{:S(2)}) collective-permute-start(bf16[512,1024]{1,0:T(8,128)(2,1)} %collective-permute-done.5), channel_id=1, source_target_pairs={{0,28},{4,0},{8,4},{12,8},{16,12},{20,16},{24,20},{28,24},{1,29},{... | collective-permute-start | bytes 3145736 | tf_op jit(solution)/shard_map/ppermute | solution.py:28
  79.2 23.4 %collective-permute-done.3 = bf16[512,1024]{1,0:T(8,128)(2,1)} collective-permute-done((bf16[512,1024]{1,0:T(8,128)(2,1)}, bf16[512,1024]{1,0:T(8,128)(2,1)}, u32[]{:S(2)}, u32[]{:S(2)}) %collective-permute-start.3) | collective-permute-done | bytes 1048608 | tf_op jit(solution)/shard_map/ppermute | solution.py:24
  102.6 2.3 constant_dynamic-update-slice_fusion.15
  104.9 2.3 constant_dynamic-update-slice_fusion.14
  107.2 2.3 constant_dynamic-update-slice_fusion.13
  109.4 1.1 constant_dynamic-update-slice_fusion.12
  110.5 2.4 %constant_dynamic-update-slice_fusion.11 = bf16[8192,1024]{1,0:T(8,128)(2,1)} fusion(bf16[8192,1024]{1,0:T(8,128)(2,1)} %constant_dynamic-update-slice_fusion.12, bf16[512,1024]{1,0:T(8,128)(2,1)} %param.6, bf16[1024]{0:T(1024)(128)(2,1)S(1)} %convert_element_type.9), kind=kLoop, calls=%fused_computation.18 | loop fusion | flops 2097152 | bytes 2099200
  112.9 1.1 constant_dynamic-update-slice_fusion.10
  114.0 2.3 constant_dynamic-update-slice_fusion.9
  116.3 0.0 collective-permute-done.6
  116.3 1.1 constant_dynamic-update-slice_fusion.8
  117.4 2.4 %constant_dynamic-update-slice_fusion.7 = bf16[8192,1024]{1,0:T(8,128)(2,1)} fusion(bf16[8192,1024]{1,0:T(8,128)(2,1)} %constant_dynamic-update-slice_fusion.8, bf16[512,1024]{1,0:T(8,128)(2,1)} %collective-permute-done.3), kind=kLoop, calls=%fused_computation.14 | loop fusion | bytes 2097152
  119.8 2.3 constant_dynamic-update-slice_fusion.6
  122.0 0.0 copy-done.4
  122.0 1.1 constant_dynamic-update-slice_fusion.5
  123.1 1.1 constant_dynamic-update-slice_fusion.4
  124.2 0.0 copy-done
  124.2 1.3 constant_dynamic-update-slice_fusion.3
  125.5 1.1 constant_dynamic-update-slice_fusion.2
  126.5 2.3 constant_dynamic-update-slice_fusion.1
  128.8 0.0 copy-start.2
  128.8 1.0 constant_dynamic-update-slice_fusion
  129.8 0.0 copy-start.5
  129.8 32.1 %all-gather.2.cloned.1.call-done = f32[512,4096]{1,0:T(8,128)} async-done(((f32[512,1024]{1,0:T(8,128)}), f32[512,4096]{1,0:T(8,128)}) %all-gather.2.cloned.1.call-update) | async-done | bytes 8388624 | tf_op jit(solution)/shard_map/all_gather | solution.py:54
  162.0 18.9 %multiply_negate_fusion = f32[1024,512]{1,0:T(8,128)S(1)} fusion(f32[512,4096]{1,0:T(8,128)} %all-gather.2.cloned.1.call-done, bf16[8192,1024]{1,0:T(8,128)(2,1)} %constant_dynamic-update-slice_fusion, s32[]{:T(128)S(6)} %select_n.29, f32[1024]{0:T(1024)S(1)} %bitcast.20), kind=kOutput, calls=%fused_computation.2 | convolution fusion | flops 25770852352 | bytes 18878468 | tf_op jit(solution)/shard_map/dot_general | solution.py:55
  180.8 0.0 copy-done.2
  180.8 3.1 %fusion.4 = f32[2,512,512]{2,1,0:T(8,128)} fusion(f32[512,2,512]{0,2,1:T(8,128)S(1)} %bitcast.15, bf16[64,2,8,512]{3,2,1,0:T(8,128)(2,1)S(1)} %bitcast.18), kind=kOutput, calls=%fused_computation.3 | convolution fusion | flops 3221225472 | bytes 5242880 | tf_op jit(solution)/shard_map/ikc,ikd->ckd/dot_general | solution.py:61
  183.9 2.9 %copy.8 = f32[512,1024]{1,0:T(8,128)} copy(f32[512,1024]{0,1:T(8,128)} %bitcast.17) | data formatting | bytes 4194304 | tf_op jit(solution)/shard_map/reshape | solution.py:65
  186.9 0.0 reduce-scatter.2.cloned.1.call-update
  186.9 1.8 copy.9
  188.7 37.8 %reduce-scatter.2.cloned.1.call-done = f32[64,1024]{1,0:T(8,128)} async-done(((f32[512,1024]{1,0:T(8,128)}), f32[64,1024]{1,0:T(8,128)}) %reduce-scatter.2.cloned.1.call-update) | async-done | bytes 262160 | tf_op jit(solution)/shard_map/reduce_scatter | solution.py:64
  226.4 0.0 copy-done.5
  226.5 1.7 sub.17
  (2 shorter events, 0.0 us)
Async XLA Ops:
  7.2 117.0 %copy-start = (bf16[512,1024]{1,0:T(8,128)(2,1)S(1)}, bf16[512,1024]{1,0:T(8,128)(2,1)}, u32[]{:S(2)}) copy-start(bf16[512,1024]{1,0:T(8,128)(2,1)} %param.6) | copy-start | bytes 3145732
  7.2 154.8 %all-gather.2.cloned.1.call-start = ((), (), s32[]{:S(2)}) async-start(), calls=%async_computation.1 | async-start | bytes 10485760 | tf_op jit(solution)/shard_map/all_gather | solution.py:54
  7.9 218.5 %reduce-scatter.2.cloned.1.call-start = ((), (), s32[]{:S(2)}) async-start(), calls=%async_computation.2 | async-start | bytes 2359296 | tf_op jit(solution)/shard_map/reduce_scatter | solution.py:64
  11.0 15.9 %copy-start.1 = (bf16[512,1024]{1,0:T(8,128)(2,1)}, bf16[512,1024]{1,0:T(8,128)(2,1)S(1)}, u32[]{:S(2)}) copy-start(bf16[512,1024]{1,0:T(8,128)(2,1)S(1)} %broadcast_multiply_fusion) | copy-start | bytes 3145732
  11.0 15.9 %collective-permute-start = (bf16[512,1024]{1,0:T(8,128)(2,1)S(1)}, bf16[512,1024]{1,0:T(8,128)(2,1)S(1)}, u32[]{:S(2)}, u32[]{:S(2)}) collective-permute-start(bf16[512,1024]{1,0:T(8,128)(2,1)S(1)} %broadcast_multiply_fusion), channel_id=1, source_target_pairs={{0,4},{4,8},{8,12},{12,16},{16,20},{20,24},{24,28},{28,0},{1,5},{5... | collective-permute-start | bytes 3145736 | tf_op jit(solution)/shard_map/ppermute | solution.py:24
  26.8 24.6 %collective-permute-start.1 = (bf16[512,1024]{1,0:T(8,128)(2,1)S(1)}, bf16[512,1024]{1,0:T(8,128)(2,1)S(1)}, u32[]{:S(2)}, u32[]{:S(2)}) collective-permute-start(bf16[512,1024]{1,0:T(8,128)(2,1)S(1)} %collective-permute-done), channel_id=1, source_target_pairs={{0,4},{4,8},{8,12},{12,16},{16,20},{20,24},{24,28},{28,0},{1,5},{5... | collective-permute-start | bytes 3145736 | tf_op jit(solution)/shard_map/ppermute | solution.py:24
  26.8 24.6 %collective-permute-start.4 = (bf16[512,1024]{1,0:T(8,128)(2,1)S(1)}, bf16[512,1024]{1,0:T(8,128)(2,1)S(1)}, u32[]{:S(2)}, u32[]{:S(2)}) collective-permute-start(bf16[512,1024]{1,0:T(8,128)(2,1)S(1)} %broadcast_multiply_fusion), channel_id=1, source_target_pairs={{0,28},{4,0},{8,4},{12,8},{16,12},{20,16},{24,20},{28,24},{1,29},{... | collective-permute-start | bytes 3145736 | tf_op jit(solution)/shard_map/ppermute | solution.py:28
  51.4 1.0 copy-start.3
  51.4 25.2 %collective-permute-start.2 = (bf16[512,1024]{1,0:T(8,128)(2,1)S(1)}, bf16[512,1024]{1,0:T(8,128)(2,1)}, u32[]{:S(2)}, u32[]{:S(2)}) collective-permute-start(bf16[512,1024]{1,0:T(8,128)(2,1)S(1)} %collective-permute-done.1), channel_id=1, source_target_pairs={{0,4},{4,8},{8,12},{12,16},{16,20},{20,24},{24,28},{28,0},{1,5},{5... | collective-permute-start | bytes 3145736 | tf_op jit(solution)/shard_map/ppermute | solution.py:24
  52.4 24.2 %collective-permute-start.5 = (bf16[512,1024]{1,0:T(8,128)(2,1)S(1)}, bf16[512,1024]{1,0:T(8,128)(2,1)}, u32[]{:S(2)}, u32[]{:S(2)}) collective-permute-start(bf16[512,1024]{1,0:T(8,128)(2,1)S(1)} %collective-permute-done.4), channel_id=1, source_target_pairs={{0,28},{4,0},{8,4},{12,8},{16,12},{20,16},{24,20},{28,24},{1,29},{... | collective-permute-start | bytes 3145736 | tf_op jit(solution)/shard_map/ppermute | solution.py:28
  76.6 26.0 %collective-permute-start.3 = (bf16[512,1024]{1,0:T(8,128)(2,1)}, bf16[512,1024]{1,0:T(8,128)(2,1)}, u32[]{:S(2)}, u32[]{:S(2)}) collective-permute-start(bf16[512,1024]{1,0:T(8,128)(2,1)} %collective-permute-done.2), channel_id=1, source_target_pairs={{0,4},{4,8},{8,12},{12,16},{16,20},{20,24},{24,28},{28,0},{1,5},{5... | collective-permute-start | bytes 3145736 | tf_op jit(solution)/shard_map/ppermute | solution.py:24
  76.6 45.4 %copy-start.4 = (bf16[512,1024]{1,0:T(8,128)(2,1)S(1)}, bf16[512,1024]{1,0:T(8,128)(2,1)}, u32[]{:S(2)}) copy-start(bf16[512,1024]{1,0:T(8,128)(2,1)} %copy-done.3) | copy-start | bytes 3145732
  76.6 39.7 %collective-permute-start.6 = (bf16[512,1024]{1,0:T(8,128)(2,1)}, bf16[512,1024]{1,0:T(8,128)(2,1)S(1)}, u32[]{:S(2)}, u32[]{:S(2)}) collective-permute-start(bf16[512,1024]{1,0:T(8,128)(2,1)} %collective-permute-done.5), channel_id=1, source_target_pairs={{0,28},{4,0},{8,4},{12,8},{16,12},{20,16},{24,20},{28,24},{1,29},{... | collective-permute-start | bytes 3145736 | tf_op jit(solution)/shard_map/ppermute | solution.py:28
  128.8 52.0 %copy-start.2 = (bf16[512,1024]{1,0:T(8,128)(2,1)S(1)}, bf16[512,1024]{1,0:T(8,128)(2,1)}, u32[]{:S(2)}) copy-start(bf16[512,1024]{1,0:T(8,128)(2,1)} %copy-done.1) | copy-start | bytes 3145732
  129.8 96.6 %copy-start.5 = (f32[64,1024]{1,0:T(8,128)S(1)}, f32[64,1024]{1,0:T(8,128)}, u32[]{:S(2)}) copy-start(f32[64,1024]{1,0:T(8,128)} %param.7) | copy-start | bytes 786436
Sparse Core Ops, SparseCore 0:
  9.6 152.3 all-gather.1
  187.0 39.4 reduce-scatter.1
